TPU v7x, 128 devices: a whole 4x4x4 slice. The times are simulated.
128 devices in a mesh: row: 8 (over x, y_lo), col: 8 (over z, core), band: 2 (over y_hi).
Axes of the slice: x: 4, y: 4 (y_hi: 2, y_lo: 2; y = y_hi * 2 + y_lo), z: 4, core: 2. Of those that a mesh axis runs over, the one named last changes fastest.
Arguments:
- freq_index: int32 [2], replicated, may hold values from 0 to 32
- band_energy: float32 [16], replicated, may hold values from -4 to 4
- pole_amp: float32 [8192, 8192], P('row', 'col'), may hold values from -6 to 6
- pole_freq: float32 [8192, 8192], P('row', 'col'), may hold values from 0.5 to 4
- left_pieces: bfloat16 [16, 256, 8192], P(('col', 'band'), None, 'row'), may hold values from -0.032958984 to 0.032958984
- right_pieces: bfloat16 [16, 256, 8192], P(('row', 'band'), None, 'col'), may hold values from -0.032958984 to 0.032958984
Outputs:
- sigma: float32 [2, 256, 256], P(None, ('row', 'col', 'band'))
All inputs are finite; a program needn't handle non-finite values.
Results may differ from a plain program's by a relative error of at most 0.0055.
Values may be sent and summed in bfloat16 or wider, within the bound.
A program may use at most 128 MiB of HBM per device.

v0:
```python
import jax
import jax.numpy as jnp
from jax import lax
from jax.sharding import Mesh
from jax.sharding import PartitionSpec as P

ROW = ("row_0", "row_1")
ROW_COL_BAND = ("row_0", "row_1", "col", "band")
ROW_BAND = ("row_0", "row_1", "band")


def whole_of(array, axes, dim):
    for axis in reversed(axes):
        array = lax.all_gather(array, axis, axis=dim, tiled=True)
    return array


def body(freq_index, band_energy, pole_amp, pole_freq, left_pieces, right_pieces):
    bpiece = left_pieces.shape[0]
    nstate = left_pieces.shape[1]
    nfreq = freq_index.shape[0]
    nband = lax.axis_size("band")
    group = lax.axis_index("band")
    freq = -4.0 + 0.25 * freq_index.astype(jnp.float32)
    right_all = whole_of(right_pieces, ROW, 0)

    def energy_at(position):
        overall = (position // bpiece * nband + group) * bpiece + position % bpiece
        return lax.dynamic_index_in_dim(band_energy, overall, 0, False)

    def add_band(total, left_band, position):
        right_band = lax.dynamic_index_in_dim(right_all, position, 0, False)
        energy = energy_at(position)
        results = []
        for w in range(nfreq):
            distance = freq[w] - energy - pole_freq
            screened = (pole_amp * distance / (distance * distance + 0.25)).astype(jnp.bfloat16)
            partial_value = jnp.dot(left_band, screened, preferred_element_type=jnp.float32).astype(
                jnp.bfloat16
            )
            results.append(
                lax.dot_general(
                    partial_value,
                    right_band,
                    (((1,), (1,)), ((), ())),
                    preferred_element_type=jnp.float32,
                )
            )
        return total + jnp.stack(results)

    start = jnp.zeros((nfreq, nstate, nstate), jnp.float32)
    left_all = lax.all_gather(left_pieces, "col", axis=0, tiled=True)

    def step(index, carry):
        left_band = lax.dynamic_index_in_dim(left_all, index, 0, False)
        return add_band(carry, left_band, index)

    total = lax.fori_loop(0, left_all.shape[0], step, start)
    summed = lax.psum(total, ROW_COL_BAND)
    owned = nstate // lax.axis_size(ROW_COL_BAND)
    sigma = lax.dynamic_slice_in_dim(summed, lax.axis_index(ROW_COL_BAND) * owned, owned, 1)
    return sigma


def solution(mesh):
    split = Mesh(
        mesh.devices.reshape(4, 2, mesh.shape["col"], mesh.shape["band"]),
        ("row_0", "row_1", "col", "band"),
    )
    in_specs = (
        P(),
        P(),
        P(ROW, "col"),
        P(ROW, "col"),
        P(("col", "band"), None, ROW),
        P(ROW_BAND, None, "col"),
    )
    out_specs = P(None, ROW_COL_BAND, None)
    return jax.shard_map(body, mesh=split, in_specs=in_specs, out_specs=out_specs, check_vma=False)
```

profile of v0, /device:TPU:1, one launch (start us, length us, event | category | flops | bytes accessed | tf_op | source)
XLA Modules:
  0.0 393.0 jit_solution(11050577234584993853)
XLA Ops:
  8.1 27.8 %all-gather.6.cloned.1.call-done = bf16[2,256,1024]{2,1,0:T(8,128)(2,1)} async-done(((bf16[1,256,1024]{2,1,0:T(8,128)(2,1)}), bf16[2,256,1024]{2,1,0:T(8,128)(2,1)}) %all-gather.6.cloned.1.call-update) | async-done | bytes 1048592 | tf_op jit(solution)/shard_map/all_gather | solution.py:14
  36.6 34.8 %all-gather.4.cloned.1.call-done = bf16[8,256,1024]{2,1,0:T(8,128)(2,1)} async-done(((bf16[1,256,1024]{2,1,0:T(8,128)(2,1)}), bf16[8,256,1024]{2,1,0:T(8,128)(2,1)}) %all-gather.4.cloned.1.call-update) | async-done | bytes 4194320 | tf_op jit(solution)/shard_map/all_gather | solution.py:52
  71.4 49.1 %all-gather.8.cloned.1.call-done = bf16[8,256,1024]{2,1,0:T(8,128)(2,1)} async-done(((bf16[2,256,1024]{2,1,0:T(8,128)(2,1)}), bf16[8,256,1024]{2,1,0:T(8,128)(2,1)}) %all-gather.8.cloned.1.call-update) | async-done | bytes 4194320 | tf_op jit(solution)/shard_map/all_gather | solution.py:14
  120.5 116.6 %while.17 = (s32[]{:T(128)}, f32[2,256,256]{2,1,0:T(8,128)S(1)}, bf16[8,256,1024]{2,1,0:T(8,128)(2,1)}, f32[2]{0:T(128)S(1)}, s32[]{:T(128)}, /*index=5*/f32[16]...) while((s32[]{:T(128)}, f32[2,256,256]{2,1,0:T(8,128)S(1)}, ...), condition=%wide.region_1.2_spmd.clone, body=%wide.region_0.1_spmd.clone.sunk | while | flops 1355677696 | bytes 20974844 | solution.py:58
  124.7 5.1 %convolution_bitcast_fusion.4 = f32[1,256,256]{2,1,0:T(8,128)S(1)} fusion(f32[1024,1024]{1,0:T(8,128)} %get-tuple-element.398, f32[1024,1024]{1,0:T(8,128)} %get-tuple-element.397, f32[]{:T(128)} %bitcast.32, bf16[8,256,1024]{2,1,0:T(8,128)(2,1)} %get-tuple-element.399, s32[]{:T(128)S(6)} %copy.9, bf16[8,256,1024]{2,1,0:T(8,128)(2,1)} %get-tuple-element.393), kind=kOutput, calls=%fused_computation.6.clone.1 | convolution fusion | flops 677642240 | bytes 9700864 | tf_op jit(solution)/shard_map/while/body/eval_jaxpr/dot_general | solution.py:42
  129.8 5.1 %convolution_bitcast_fusion.5 = f32[1,256,256]{2,1,0:T(8,128)S(1)} fusion(f32[1024,1024]{1,0:T(8,128)} %get-tuple-element.398, f32[1024,1024]{1,0:T(8,128)} %get-tuple-element.397, f32[]{:T(128)} %bitcast.33, bf16[8,256,1024]{2,1,0:T(8,128)(2,1)} %get-tuple-element.399, s32[]{:T(128)S(6)} %copy.9, bf16[8,256,1024]{2,1,0:T(8,128)(2,1)} %get-tuple-element.393), kind=kOutput, calls=%fused_computation.7.clone.1 | convolution fusion | flops 677642240 | bytes 9700864 | tf_op jit(solution)/shard_map/while/body/eval_jaxpr/dot_general | solution.py:42
  135.1 1.2 dynamic_slice.70
  139.3 5.1 %convolution_bitcast_fusion.4 = f32[1,256,256]{2,1,0:T(8,128)S(1)} fusion(f32[1024,1024]{1,0:T(8,128)} %get-tuple-element.398, f32[1024,1024]{1,0:T(8,128)} %get-tuple-element.397, f32[]{:T(128)} %bitcast.32, bf16[8,256,1024]{2,1,0:T(8,128)(2,1)} %get-tuple-element.399, s32[]{:T(128)S(6)} %copy.9, bf16[8,256,1024]{2,1,0:T(8,128)(2,1)} %get-tuple-element.393), kind=kOutput, calls=%fused_computation.6.clone.1 | convolution fusion | flops 677642240 | bytes 9700864 | tf_op jit(solution)/shard_map/while/body/eval_jaxpr/dot_general | solution.py:42
  144.4 5.1 %convolution_bitcast_fusion.5 = f32[1,256,256]{2,1,0:T(8,128)S(1)} fusion(f32[1024,1024]{1,0:T(8,128)} %get-tuple-element.398, f32[1024,1024]{1,0:T(8,128)} %get-tuple-element.397, f32[]{:T(128)} %bitcast.33, bf16[8,256,1024]{2,1,0:T(8,128)(2,1)} %get-tuple-element.399, s32[]{:T(128)S(6)} %copy.9, bf16[8,256,1024]{2,1,0:T(8,128)(2,1)} %get-tuple-element.393), kind=kOutput, calls=%fused_computation.7.clone.1 | convolution fusion | flops 677642240 | bytes 9700864 | tf_op jit(solution)/shard_map/while/body/eval_jaxpr/dot_general | solution.py:42
  149.6 1.2 dynamic_slice.70
  153.9 5.1 %convolution_bitcast_fusion.4 = f32[1,256,256]{2,1,0:T(8,128)S(1)} fusion(f32[1024,1024]{1,0:T(8,128)} %get-tuple-element.398, f32[1024,1024]{1,0:T(8,128)} %get-tuple-element.397, f32[]{:T(128)} %bitcast.32, bf16[8,256,1024]{2,1,0:T(8,128)(2,1)} %get-tuple-element.399, s32[]{:T(128)S(6)} %copy.9, bf16[8,256,1024]{2,1,0:T(8,128)(2,1)} %get-tuple-element.393), kind=kOutput, calls=%fused_computation.6.clone.1 | convolution fusion | flops 677642240 | bytes 9700864 | tf_op jit(solution)/shard_map/while/body/eval_jaxpr/dot_general | solution.py:42
  159.0 5.1 %convolution_bitcast_fusion.5 = f32[1,256,256]{2,1,0:T(8,128)S(1)} fusion(f32[1024,1024]{1,0:T(8,128)} %get-tuple-element.398, f32[1024,1024]{1,0:T(8,128)} %get-tuple-element.397, f32[]{:T(128)} %bitcast.33, bf16[8,256,1024]{2,1,0:T(8,128)(2,1)} %get-tuple-element.399, s32[]{:T(128)S(6)} %copy.9, bf16[8,256,1024]{2,1,0:T(8,128)(2,1)} %get-tuple-element.393), kind=kOutput, calls=%fused_computation.7.clone.1 | convolution fusion | flops 677642240 | bytes 9700864 | tf_op jit(solution)/shard_map/while/body/eval_jaxpr/dot_general | solution.py:42
  168.5 5.1 %convolution_bitcast_fusion.4 = f32[1,256,256]{2,1,0:T(8,128)S(1)} fusion(f32[1024,1024]{1,0:T(8,128)} %get-tuple-element.398, f32[1024,1024]{1,0:T(8,128)} %get-tuple-element.397, f32[]{:T(128)} %bitcast.32, bf16[8,256,1024]{2,1,0:T(8,128)(2,1)} %get-tuple-element.399, s32[]{:T(128)S(6)} %copy.9, bf16[8,256,1024]{2,1,0:T(8,128)(2,1)} %get-tuple-element.393), kind=kOutput, calls=%fused_computation.6.clone.1 | convolution fusion | flops 677642240 | bytes 9700864 | tf_op jit(solution)/shard_map/while/body/eval_jaxpr/dot_general | solution.py:42
  173.5 5.1 %convolution_bitcast_fusion.5 = f32[1,256,256]{2,1,0:T(8,128)S(1)} fusion(f32[1024,1024]{1,0:T(8,128)} %get-tuple-element.398, f32[1024,1024]{1,0:T(8,128)} %get-tuple-element.397, f32[]{:T(128)} %bitcast.33, bf16[8,256,1024]{2,1,0:T(8,128)(2,1)} %get-tuple-element.399, s32[]{:T(128)S(6)} %copy.9, bf16[8,256,1024]{2,1,0:T(8,128)(2,1)} %get-tuple-element.393), kind=kOutput, calls=%fused_computation.7.clone.1 | convolution fusion | flops 677642240 | bytes 9700864 | tf_op jit(solution)/shard_map/while/body/eval_jaxpr/dot_general | solution.py:42
  183.0 5.1 %convolution_bitcast_fusion.4 = f32[1,256,256]{2,1,0:T(8,128)S(1)} fusion(f32[1024,1024]{1,0:T(8,128)} %get-tuple-element.398, f32[1024,1024]{1,0:T(8,128)} %get-tuple-element.397, f32[]{:T(128)} %bitcast.32, bf16[8,256,1024]{2,1,0:T(8,128)(2,1)} %get-tuple-element.399, s32[]{:T(128)S(6)} %copy.9, bf16[8,256,1024]{2,1,0:T(8,128)(2,1)} %get-tuple-element.393), kind=kOutput, calls=%fused_computation.6.clone.1 | convolution fusion | flops 677642240 | bytes 9700864 | tf_op jit(solution)/shard_map/while/body/eval_jaxpr/dot_general | solution.py:42
  188.1 5.1 %convolution_bitcast_fusion.5 = f32[1,256,256]{2,1,0:T(8,128)S(1)} fusion(f32[1024,1024]{1,0:T(8,128)} %get-tuple-element.398, f32[1024,1024]{1,0:T(8,128)} %get-tuple-element.397, f32[]{:T(128)} %bitcast.33, bf16[8,256,1024]{2,1,0:T(8,128)(2,1)} %get-tuple-element.399, s32[]{:T(128)S(6)} %copy.9, bf16[8,256,1024]{2,1,0:T(8,128)(2,1)} %get-tuple-element.393), kind=kOutput, calls=%fused_computation.7.clone.1 | convolution fusion | flops 677642240 | bytes 9700864 | tf_op jit(solution)/shard_map/while/body/eval_jaxpr/dot_general | solution.py:42
  197.6 5.1 %convolution_bitcast_fusion.4 = f32[1,256,256]{2,1,0:T(8,128)S(1)} fusion(f32[1024,1024]{1,0:T(8,128)} %get-tuple-element.398, f32[1024,1024]{1,0:T(8,128)} %get-tuple-element.397, f32[]{:T(128)} %bitcast.32, bf16[8,256,1024]{2,1,0:T(8,128)(2,1)} %get-tuple-element.399, s32[]{:T(128)S(6)} %copy.9, bf16[8,256,1024]{2,1,0:T(8,128)(2,1)} %get-tuple-element.393), kind=kOutput, calls=%fused_computation.6.clone.1 | convolution fusion | flops 677642240 | bytes 9700864 | tf_op jit(solution)/shard_map/while/body/eval_jaxpr/dot_general | solution.py:42
  202.7 5.1 %convolution_bitcast_fusion.5 = f32[1,256,256]{2,1,0:T(8,128)S(1)} fusion(f32[1024,1024]{1,0:T(8,128)} %get-tuple-element.398, f32[1024,1024]{1,0:T(8,128)} %get-tuple-element.397, f32[]{:T(128)} %bitcast.33, bf16[8,256,1024]{2,1,0:T(8,128)(2,1)} %get-tuple-element.399, s32[]{:T(128)S(6)} %copy.9, bf16[8,256,1024]{2,1,0:T(8,128)(2,1)} %get-tuple-element.393), kind=kOutput, calls=%fused_computation.7.clone.1 | convolution fusion | flops 677642240 | bytes 9700864 | tf_op jit(solution)/shard_map/while/body/eval_jaxpr/dot_general | solution.py:42
  212.2 5.1 %convolution_bitcast_fusion.4 = f32[1,256,256]{2,1,0:T(8,128)S(1)} fusion(f32[1024,1024]{1,0:T(8,128)} %get-tuple-element.398, f32[1024,1024]{1,0:T(8,128)} %get-tuple-element.397, f32[]{:T(128)} %bitcast.32, bf16[8,256,1024]{2,1,0:T(8,128)(2,1)} %get-tuple-element.399, s32[]{:T(128)S(6)} %copy.9, bf16[8,256,1024]{2,1,0:T(8,128)(2,1)} %get-tuple-element.393), kind=kOutput, calls=%fused_computation.6.clone.1 | convolution fusion | flops 677642240 | bytes 9700864 | tf_op jit(solution)/shard_map/while/body/eval_jaxpr/dot_general | solution.py:42
  217.3 5.1 %convolution_bitcast_fusion.5 = f32[1,256,256]{2,1,0:T(8,128)S(1)} fusion(f32[1024,1024]{1,0:T(8,128)} %get-tuple-element.398, f32[1024,1024]{1,0:T(8,128)} %get-tuple-element.397, f32[]{:T(128)} %bitcast.33, bf16[8,256,1024]{2,1,0:T(8,128)(2,1)} %get-tuple-element.399, s32[]{:T(128)S(6)} %copy.9, bf16[8,256,1024]{2,1,0:T(8,128)(2,1)} %get-tuple-element.393), kind=kOutput, calls=%fused_computation.7.clone.1 | convolution fusion | flops 677642240 | bytes 9700864 | tf_op jit(solution)/shard_map/while/body/eval_jaxpr/dot_general | solution.py:42
  226.8 5.1 %convolution_bitcast_fusion.4 = f32[1,256,256]{2,1,0:T(8,128)S(1)} fusion(f32[1024,1024]{1,0:T(8,128)} %get-tuple-element.398, f32[1024,1024]{1,0:T(8,128)} %get-tuple-element.397, f32[]{:T(128)} %bitcast.32, bf16[8,256,1024]{2,1,0:T(8,128)(2,1)} %get-tuple-element.399, s32[]{:T(128)S(6)} %copy.9, bf16[8,256,1024]{2,1,0:T(8,128)(2,1)} %get-tuple-element.393), kind=kOutput, calls=%fused_computation.6.clone.1 | convolution fusion | flops 677642240 | bytes 9700864 | tf_op jit(solution)/shard_map/while/body/eval_jaxpr/dot_general | solution.py:42
  231.9 5.1 %convolution_bitcast_fusion.5 = f32[1,256,256]{2,1,0:T(8,128)S(1)} fusion(f32[1024,1024]{1,0:T(8,128)} %get-tuple-element.398, f32[1024,1024]{1,0:T(8,128)} %get-tuple-element.397, f32[]{:T(128)} %bitcast.33, bf16[8,256,1024]{2,1,0:T(8,128)(2,1)} %get-tuple-element.399, s32[]{:T(128)S(6)} %copy.9, bf16[8,256,1024]{2,1,0:T(8,128)(2,1)} %get-tuple-element.393), kind=kOutput, calls=%fused_computation.7.clone.1 | convolution fusion | flops 677642240 | bytes 9700864 | tf_op jit(solution)/shard_map/while/body/eval_jaxpr/dot_general | solution.py:42
  237.9 147.2 %all-reduce.2.cloned.1.call-done = f32[2,256,256]{2,1,0:T(8,128)} async-done(((f32[2,256,256]{2,1,0:T(8,128)}), f32[2,256,256]{2,1,0:T(8,128)}) %all-reduce.2.cloned.1.call-update) | async-done | bytes 524304 | tf_op jit(solution)/shard_map/psum | solution.py:59
  385.1 1.3 constant_dynamic-slice_fusion
  (34 shorter events, 16.7 us)
Async XLA Ops:
  6.5 29.3 %all-gather.6.cloned.1.call-start = ((), (), s32[]{:S(2)}) async-start(), calls=%async_computation.1 | async-start | bytes 1572864 | tf_op jit(solution)/shard_map/all_gather | solution.py:14
  7.3 64.2 %all-gather.4.cloned.1.call-start = ((), (), s32[]{:S(2)}) async-start(), calls=%async_computation | async-start | bytes 4718592 | tf_op jit(solution)/shard_map/all_gather | solution.py:52
  8.0 112.5 %all-gather.8.cloned.1.call-start = ((), (), s32[]{:S(2)}) async-start(), calls=%async_computation.2 | async-start | bytes 5242880 | tf_op jit(solution)/shard_map/all_gather | solution.py:14
  35.9 349.2 %all-reduce.2.cloned.1.call-start = ((), (), s32[]{:S(2)}) async-start(), calls=%async_computation.3 | async-start | bytes 1048576 | tf_op jit(solution)/shard_map/psum | solution.py:59
  237.1 0.8 copy-start
Sparse Core Ops, SparseCore 0:
  9.0 26.8 all-gather.5
  37.6 33.7 all-gather.3
  73.1 47.3 all-gather.7
  238.0 147.0 all-reduce.1
where the time goes:
time: 393 us
  waiting for transfers between devices  260 us (66%)
  matrix products  81.2 us (21%)
  loops' own time  19.2 us (5%)
  local copies, waits for them, and re-layouts  17.1 us (4%)
  between operations  13.2 us (3%)
    psum x1, waiting for transfers between devices, body(): summed = lax.psum(total, ROW_COL_BAND)  147 us
    dot_general x16, matrix products, add_band(): lax.dot_general(partial_value, right_band, (((1,), (1,)), ((), ())), pref...  81.2 us
    all_gather x2, waiting for transfers between devices, whole_of(): array = lax.all_gather(array, axis, axis=dim, tiled=True)  76.9 us
    all_gather x1, waiting for transfers between devices, body(): left_all = lax.all_gather(left_pieces, 'col', axis=0, tiled=True)  34.8 us
    another operation x1, loops' own time, body(): total = lax.fori_loop(0, left_all.shape[0], step, start)  19.2 us
    dynamic_slice x8, local copies, waits for them, and re-layouts, energy_at(): return lax.dynamic_index_in_dim(band_energy, overall, 0, False)  9.87 us
  transfers between devices with their start and end apart: 4, of which 4 were waited for; matrix products, arithmetic and copies ran while one was open for 0% of the time, Pallas kernels for 0%

commit v1 on v0

--- a/solution.py
+++ b/solution.py
@@ -49,7 +49,15 @@
         return total + jnp.stack(results)
 
     start = jnp.zeros((nfreq, nstate, nstate), jnp.float32)
-    left_all = lax.all_gather(left_pieces, "col", axis=0, tiled=True)
+    left_all = jnp.concatenate(
+        lax.all_to_all(
+            jnp.stack([left_pieces] * lax.psum(1, axis_name="col"), axis=0),
+            axis_name="col",
+            split_axis=0,
+            concat_axis=0,
+        ),
+        axis=0,
+    )
 
     def step(index, carry):
         left_band = lax.dynamic_index_in_dim(left_all, index, 0, False)

time: 393 us -> 360 us (0.916)
  waiting for transfers between devices: 260 us -> 224 us
  starting transfers between devices: 0.12 us -> 5.44 us
    all_to_all x0 -> x1, waiting for transfers between devices: none -> 48.8 us  [body(): lax.all_to_all(jnp.stack([left_pieces] * lax.psum(1, axis_name='col'), ax...]
    all_gather x2, waiting for transfers between devices: 76.9 us -> 28.6 us  [whole_of(): array = lax.all_gather(array, axis, axis=dim, tiled=True)]
    all_gather x1 -> x0, waiting for transfers between devices: 34.8 us -> none  [body(): left_all = lax.all_gather(left_pieces, 'col', axis=0, tiled=True)]
    all_to_all x0 -> x1, starting transfers between devices: none -> 5.39 us  [body(): lax.all_to_all(jnp.stack([left_pieces] * lax.psum(1, axis_name='col'), ax...]
    dynamic_slice x8, local copies, waits for them, and re-layouts: 9.87 us -> 4.63 us  [energy_at(): return lax.dynamic_index_in_dim(band_energy, overall, 0, False)]
  transfers between devices with their start and end apart: 4 -> 4, of which waited for: 4 -> 3; matrix products, arithmetic and copies ran while one was open for 0% -> 1% of each run, Pallas kernels for 0% -> 0%
where the time goes in v1:
time: 360 us
  waiting for transfers between devices  224 us (62%)
  matrix products  81 us (22%)
  loops' own time  19.3 us (5%)
  local copies, waits for them, and re-layouts  15.4 us (4%)
  between operations  13.1 us (4%)
  starting transfers between devices  5.44 us (2%)
    psum x1, waiting for transfers between devices, body(): summed = lax.psum(total, ROW_COL_BAND)  146 us
    dot_general x16, matrix products, add_band(): lax.dot_general(partial_value, right_band, (((1,), (1,)), ((), ())), pref...  81 us
    all_to_all x1, waiting for transfers between devices, body(): lax.all_to_all(jnp.stack([left_pieces] * lax.psum(1, axis_name='col'), ax...  48.8 us
    all_gather x2, waiting for transfers between devices, whole_of(): array = lax.all_gather(array, axis, axis=dim, tiled=True)  28.6 us
    another operation x1, loops' own time, body(): total = lax.fori_loop(0, left_all.shape[0], step, start)  19.3 us
  transfers between devices with their start and end apart: 4, of which 3 were waited for; matrix products, arithmetic and copies ran while one was open for 1% of the time, Pallas kernels for 0%

profile of v1, /device:TPU:1, one launch (start us, length us, event | category | flops | bytes accessed | tf_op | source)
XLA Modules:
  0.0 359.6 jit_solution(10050549751825338046)
XLA Ops:
  7.3 28.6 %all-gather.3.cloned.1.call-done = bf16[2,256,1024]{2,1,0:T(8,128)(2,1)} async-done(((bf16[1,256,1024]{2,1,0:T(8,128)(2,1)}), bf16[2,256,1024]{2,1,0:T(8,128)(2,1)}) %all-gather.3.cloned.1.call-update) | async-done | bytes 1048592 | tf_op jit(solution)/shard_map/all_gather | solution.py:14
  35.9 3.5 stack.44
  39.4 5.4 %all-to-all-start = ((bf16[8,1,256,1024]{3,2,1,0:T(8,128)(2,1)}), bf16[8,1,256,1024]{3,2,1,0:T(8,128)(2,1)}, u32[]{:S(2)}, u32[]{:S(2)}) async-start(bf16[8,1,256,1024]{3,2,1,0:T(8,128)(2,1)} %stack.44), calls=%async_computation | async-start | bytes 8388608 | tf_op jit(solution)/shard_map/all_to_all | solution.py:53
  44.9 48.8 %all-to-all-done = bf16[8,1,256,1024]{3,2,1,0:T(8,128)(2,1)} async-done(((bf16[8,1,256,1024]{3,2,1,0:T(8,128)(2,1)}), bf16[8,1,256,1024]{3,2,1,0:T(8,128)(2,1)}, u32[]{:S(2)}, u32[]{:S(2)}) %all-to-all-start) | async-done | bytes 4194336 | tf_op jit(solution)/shard_map/all_to_all | solution.py:53
  93.6 111.3 %while.17 = (s32[]{:T(128)}, f32[2,256,256]{2,1,0:T(8,128)S(1)}, bf16[8,256,1024]{2,1,0:T(8,128)(2,1)}, f32[2]{0:T(128)S(1)}, s32[]{:T(128)}, /*index=5*/f32[16]...) while((s32[]{:T(128)}, f32[2,256,256]{2,1,0:T(8,128)S(1)}, ...), condition=%wide.region_1.2_spmd.clone, body=%wide.region_0.1_spmd.clone.sunk | while | flops 1355677696 | bytes 20974836 | solution.py:66
  96.0 5.1 %convolution_bitcast_fusion.5 = f32[1,256,256]{2,1,0:T(8,128)S(1)} fusion(f32[1024,1024]{1,0:T(8,128)} %get-tuple-element.398, f32[1024,1024]{1,0:T(8,128)} %get-tuple-element.397, f32[]{:T(128)} %bitcast.35, bf16[8,256,1024]{2,1,0:T(8,128)(2,1)} %get-tuple-element.399, s32[]{:T(128)} %get-tuple-element.378, bf16[8,256,1024]{2,1,0:T(8,128)(2,1)} %get-tuple-element.393), kind=kOutput, calls=%fused_computation.7.clone.1 | convolution fusion | flops 677642240 | bytes 9700864 | tf_op jit(solution)/shard_map/while/body/eval_jaxpr/dot_general | solution.py:42
  102.3 5.1 %convolution_bitcast_fusion.4 = f32[1,256,256]{2,1,0:T(8,128)S(1)} fusion(f32[1024,1024]{1,0:T(8,128)} %get-tuple-element.398, f32[1024,1024]{1,0:T(8,128)} %get-tuple-element.397, f32[]{:T(128)} %bitcast.34, bf16[8,256,1024]{2,1,0:T(8,128)(2,1)} %get-tuple-element.399, s32[]{:T(128)} %get-tuple-element.378, bf16[8,256,1024]{2,1,0:T(8,128)(2,1)} %get-tuple-element.393), kind=kOutput, calls=%fused_computation.6.clone.1 | convolution fusion | flops 677642240 | bytes 9700864 | tf_op jit(solution)/shard_map/while/body/eval_jaxpr/dot_general | solution.py:42
  110.0 5.1 %convolution_bitcast_fusion.5 = f32[1,256,256]{2,1,0:T(8,128)S(1)} fusion(f32[1024,1024]{1,0:T(8,128)} %get-tuple-element.398, f32[1024,1024]{1,0:T(8,128)} %get-tuple-element.397, f32[]{:T(128)} %bitcast.35, bf16[8,256,1024]{2,1,0:T(8,128)(2,1)} %get-tuple-element.399, s32[]{:T(128)} %get-tuple-element.378, bf16[8,256,1024]{2,1,0:T(8,128)(2,1)} %get-tuple-element.393), kind=kOutput, calls=%fused_computation.7.clone.1 | convolution fusion | flops 677642240 | bytes 9700864 | tf_op jit(solution)/shard_map/while/body/eval_jaxpr/dot_general | solution.py:42
  116.2 5.1 %convolution_bitcast_fusion.4 = f32[1,256,256]{2,1,0:T(8,128)S(1)} fusion(f32[1024,1024]{1,0:T(8,128)} %get-tuple-element.398, f32[1024,1024]{1,0:T(8,128)} %get-tuple-element.397, f32[]{:T(128)} %bitcast.34, bf16[8,256,1024]{2,1,0:T(8,128)(2,1)} %get-tuple-element.399, s32[]{:T(128)} %get-tuple-element.378, bf16[8,256,1024]{2,1,0:T(8,128)(2,1)} %get-tuple-element.393), kind=kOutput, calls=%fused_computation.6.clone.1 | convolution fusion | flops 677642240 | bytes 9700864 | tf_op jit(solution)/shard_map/while/body/eval_jaxpr/dot_general | solution.py:42
  123.9 5.1 %convolution_bitcast_fusion.5 = f32[1,256,256]{2,1,0:T(8,128)S(1)} fusion(f32[1024,1024]{1,0:T(8,128)} %get-tuple-element.398, f32[1024,1024]{1,0:T(8,128)} %get-tuple-element.397, f32[]{:T(128)} %bitcast.35, bf16[8,256,1024]{2,1,0:T(8,128)(2,1)} %get-tuple-element.399, s32[]{:T(128)} %get-tuple-element.378, bf16[8,256,1024]{2,1,0:T(8,128)(2,1)} %get-tuple-element.393), kind=kOutput, calls=%fused_computation.7.clone.1 | convolution fusion | flops 677642240 | bytes 9700864 | tf_op jit(solution)/shard_map/while/body/eval_jaxpr/dot_general | solution.py:42
  130.1 5.1 %convolution_bitcast_fusion.4 = f32[1,256,256]{2,1,0:T(8,128)S(1)} fusion(f32[1024,1024]{1,0:T(8,128)} %get-tuple-element.398, f32[1024,1024]{1,0:T(8,128)} %get-tuple-element.397, f32[]{:T(128)} %bitcast.34, bf16[8,256,1024]{2,1,0:T(8,128)(2,1)} %get-tuple-element.399, s32[]{:T(128)} %get-tuple-element.378, bf16[8,256,1024]{2,1,0:T(8,128)(2,1)} %get-tuple-element.393), kind=kOutput, calls=%fused_computation.6.clone.1 | convolution fusion | flops 677642240 | bytes 9700864 | tf_op jit(solution)/shard_map/while/body/eval_jaxpr/dot_general | solution.py:42
  137.8 5.1 %convolution_bitcast_fusion.5 = f32[1,256,256]{2,1,0:T(8,128)S(1)} fusion(f32[1024,1024]{1,0:T(8,128)} %get-tuple-element.398, f32[1024,1024]{1,0:T(8,128)} %get-tuple-element.397, f32[]{:T(128)} %bitcast.35, bf16[8,256,1024]{2,1,0:T(8,128)(2,1)} %get-tuple-element.399, s32[]{:T(128)} %get-tuple-element.378, bf16[8,256,1024]{2,1,0:T(8,128)(2,1)} %get-tuple-element.393), kind=kOutput, calls=%fused_computation.7.clone.1 | convolution fusion | flops 677642240 | bytes 9700864 | tf_op jit(solution)/shard_map/while/body/eval_jaxpr/dot_general | solution.py:42
  144.0 5.1 %convolution_bitcast_fusion.4 = f32[1,256,256]{2,1,0:T(8,128)S(1)} fusion(f32[1024,1024]{1,0:T(8,128)} %get-tuple-element.398, f32[1024,1024]{1,0:T(8,128)} %get-tuple-element.397, f32[]{:T(128)} %bitcast.34, bf16[8,256,1024]{2,1,0:T(8,128)(2,1)} %get-tuple-element.399, s32[]{:T(128)} %get-tuple-element.378, bf16[8,256,1024]{2,1,0:T(8,128)(2,1)} %get-tuple-element.393), kind=kOutput, calls=%fused_computation.6.clone.1 | convolution fusion | flops 677642240 | bytes 9700864 | tf_op jit(solution)/shard_map/while/body/eval_jaxpr/dot_general | solution.py:42
  151.7 5.1 %convolution_bitcast_fusion.5 = f32[1,256,256]{2,1,0:T(8,128)S(1)} fusion(f32[1024,1024]{1,0:T(8,128)} %get-tuple-element.398, f32[1024,1024]{1,0:T(8,128)} %get-tuple-element.397, f32[]{:T(128)} %bitcast.35, bf16[8,256,1024]{2,1,0:T(8,128)(2,1)} %get-tuple-element.399, s32[]{:T(128)} %get-tuple-element.378, bf16[8,256,1024]{2,1,0:T(8,128)(2,1)} %get-tuple-element.393), kind=kOutput, calls=%fused_computation.7.clone.1 | convolution fusion | flops 677642240 | bytes 9700864 | tf_op jit(solution)/shard_map/while/body/eval_jaxpr/dot_general | solution.py:42
  157.9 5.1 %convolution_bitcast_fusion.4 = f32[1,256,256]{2,1,0:T(8,128)S(1)} fusion(f32[1024,1024]{1,0:T(8,128)} %get-tuple-element.398, f32[1024,1024]{1,0:T(8,128)} %get-tuple-element.397, f32[]{:T(128)} %bitcast.34, bf16[8,256,1024]{2,1,0:T(8,128)(2,1)} %get-tuple-element.399, s32[]{:T(128)} %get-tuple-element.378, bf16[8,256,1024]{2,1,0:T(8,128)(2,1)} %get-tuple-element.393), kind=kOutput, calls=%fused_computation.6.clone.1 | convolution fusion | flops 677642240 | bytes 9700864 | tf_op jit(solution)/shard_map/while/body/eval_jaxpr/dot_general | solution.py:42
  165.6 5.1 %convolution_bitcast_fusion.5 = f32[1,256,256]{2,1,0:T(8,128)S(1)} fusion(f32[1024,1024]{1,0:T(8,128)} %get-tuple-element.398, f32[1024,1024]{1,0:T(8,128)} %get-tuple-element.397, f32[]{:T(128)} %bitcast.35, bf16[8,256,1024]{2,1,0:T(8,128)(2,1)} %get-tuple-element.399, s32[]{:T(128)} %get-tuple-element.378, bf16[8,256,1024]{2,1,0:T(8,128)(2,1)} %get-tuple-element.393), kind=kOutput, calls=%fused_computation.7.clone.1 | convolution fusion | flops 677642240 | bytes 9700864 | tf_op jit(solution)/shard_map/while/body/eval_jaxpr/dot_general | solution.py:42
  171.9 5.1 %convolution_bitcast_fusion.4 = f32[1,256,256]{2,1,0:T(8,128)S(1)} fusion(f32[1024,1024]{1,0:T(8,128)} %get-tuple-element.398, f32[1024,1024]{1,0:T(8,128)} %get-tuple-element.397, f32[]{:T(128)} %bitcast.34, bf16[8,256,1024]{2,1,0:T(8,128)(2,1)} %get-tuple-element.399, s32[]{:T(128)} %get-tuple-element.378, bf16[8,256,1024]{2,1,0:T(8,128)(2,1)} %get-tuple-element.393), kind=kOutput, calls=%fused_computation.6.clone.1 | convolution fusion | flops 677642240 | bytes 9700864 | tf_op jit(solution)/shard_map/while/body/eval_jaxpr/dot_general | solution.py:42
  179.5 5.1 %convolution_bitcast_fusion.5 = f32[1,256,256]{2,1,0:T(8,128)S(1)} fusion(f32[1024,1024]{1,0:T(8,128)} %get-tuple-element.398, f32[1024,1024]{1,0:T(8,128)} %get-tuple-element.397, f32[]{:T(128)} %bitcast.35, bf16[8,256,1024]{2,1,0:T(8,128)(2,1)} %get-tuple-element.399, s32[]{:T(128)} %get-tuple-element.378, bf16[8,256,1024]{2,1,0:T(8,128)(2,1)} %get-tuple-element.393), kind=kOutput, calls=%fused_computation.7.clone.1 | convolution fusion | flops 677642240 | bytes 9700864 | tf_op jit(solution)/shard_map/while/body/eval_jaxpr/dot_general | solution.py:42
  185.8 5.1 %convolution_bitcast_fusion.4 = f32[1,256,256]{2,1,0:T(8,128)S(1)} fusion(f32[1024,1024]{1,0:T(8,128)} %get-tuple-element.398, f32[1024,1024]{1,0:T(8,128)} %get-tuple-element.397, f32[]{:T(128)} %bitcast.34, bf16[8,256,1024]{2,1,0:T(8,128)(2,1)} %get-tuple-element.399, s32[]{:T(128)} %get-tuple-element.378, bf16[8,256,1024]{2,1,0:T(8,128)(2,1)} %get-tuple-element.393), kind=kOutput, calls=%fused_computation.6.clone.1 | convolution fusion | flops 677642240 | bytes 9700864 | tf_op jit(solution)/shard_map/while/body/eval_jaxpr/dot_general | solution.py:42
  193.4 5.1 %convolution_bitcast_fusion.5 = f32[1,256,256]{2,1,0:T(8,128)S(1)} fusion(f32[1024,1024]{1,0:T(8,128)} %get-tuple-element.398, f32[1024,1024]{1,0:T(8,128)} %get-tuple-element.397, f32[]{:T(128)} %bitcast.35, bf16[8,256,1024]{2,1,0:T(8,128)(2,1)} %get-tuple-element.399, s32[]{:T(128)} %get-tuple-element.378, bf16[8,256,1024]{2,1,0:T(8,128)(2,1)} %get-tuple-element.393), kind=kOutput, calls=%fused_computation.7.clone.1 | convolution fusion | flops 677642240 | bytes 9700864 | tf_op jit(solution)/shard_map/while/body/eval_jaxpr/dot_general | solution.py:42
  199.7 5.1 %convolution_bitcast_fusion.4 = f32[1,256,256]{2,1,0:T(8,128)S(1)} fusion(f32[1024,1024]{1,0:T(8,128)} %get-tuple-element.398, f32[1024,1024]{1,0:T(8,128)} %get-tuple-element.397, f32[]{:T(128)} %bitcast.34, bf16[8,256,1024]{2,1,0:T(8,128)(2,1)} %get-tuple-element.399, s32[]{:T(128)} %get-tuple-element.378, bf16[8,256,1024]{2,1,0:T(8,128)(2,1)} %get-tuple-element.393), kind=kOutput, calls=%fused_computation.6.clone.1 | convolution fusion | flops 677642240 | bytes 9700864 | tf_op jit(solution)/shard_map/while/body/eval_jaxpr/dot_general | solution.py:42
  204.9 0.8 copy-done
  205.7 146.0 %all-reduce.2.cloned.1.call-done = f32[2,256,256]{2,1,0:T(8,128)} async-done(((f32[2,256,256]{2,1,0:T(8,128)}), f32[2,256,256]{2,1,0:T(8,128)}) %all-reduce.2.cloned.1.call-update) | async-done | bytes 524304 | tf_op jit(solution)/shard_map/psum | solution.py:67
  351.8 1.3 constant_dynamic-slice_fusion
  (38 shorter events, 11.8 us)
Async XLA Ops:
  6.5 29.3 %all-gather.3.cloned.1.call-start = ((), (), s32[]{:S(2)}) async-start(), calls=%async_computation.1 | async-start | bytes 1572864 | tf_op jit(solution)/shard_map/all_gather | solution.py:14
  7.3 86.4 %all-gather.5.cloned.1.call-start = ((), (), s32[]{:S(2)}) async-start(), calls=%async_computation.2 | async-start | bytes 5242880 | tf_op jit(solution)/shard_map/all_gather | solution.py:14
  39.4 5.4 %copy-start.1 = (s32[2]{0:T(128)S(1)}, s32[2]{0:T(128)}, u32[]{:S(2)}) copy-start(s32[2]{0:T(128)} %param.8) | copy-start | bytes 28
  39.4 54.2 %copy-start.2 = (f32[16]{0:T(128)S(1)}, f32[16]{0:T(128)}, u32[]{:S(2)}) copy-start(f32[16]{0:T(128)} %param.9) | copy-start | bytes 196
  39.4 54.2 %all-to-all-start = ((bf16[8,1,256,1024]{3,2,1,0:T(8,128)(2,1)}), bf16[8,1,256,1024]{3,2,1,0:T(8,128)(2,1)}, u32[]{:S(2)}, u32[]{:S(2)}) async-start(bf16[8,1,256,1024]{3,2,1,0:T(8,128)(2,1)} %stack.44), calls=%async_computation | async-start | bytes 8388608 | tf_op jit(solution)/shard_map/all_to_all | solution.py:53
  44.8 306.9 %all-reduce.2.cloned.1.call-start = ((), (), s32[]{:S(2)}) async-start(), calls=%async_computation.3 | async-start | bytes 1048576 | tf_op jit(solution)/shard_map/psum | solution.py:67
  204.9 0.8 copy-start
Sparse Core Ops, SparseCore 0:
  9.0 26.8 all-gather.2
  37.5 49.1 all-gather.4
  205.8 145.8 all-reduce.1
